TPU v7x, 512 devices: a whole 4x8x8 slice. The times are simulated.
512 devices in a mesh: expert: 64 (over y, x, core), hidden: 8 (over z).
Axes of the slice: x: 4, y: 8, z: 8, core: 2. Of those that a mesh axis runs over, the one named last changes fastest.
Arguments:
- tokens: bfloat16 [4096, 4096], P('expert', 'hidden'), may hold values from -6 to 6
- expert_ids: int32 [4096, 8], P('expert'), may hold values from 0 to 63, all different within a row; in each aligned block of 64 rows (0 to 63, 64 to 127, ...) at most 16 rows name the same one
- gate_weights: float32 [4096, 8], P('expert'), may hold values from 0.05 to 0.5
- gate_proj: bfloat16 [64, 1536, 4096], P('expert', 'hidden'), may hold values from -0.09375 to 0.09375
- up_proj: bfloat16 [64, 1536, 4096], P('expert', 'hidden'), may hold values from -0.09375 to 0.09375
- down_proj: bfloat16 [64, 1536, 4096], P('expert', None, 'hidden'), may hold values from -0.15625 to 0.15625
Outputs:
- moe_out: bfloat16 [4096, 4096], P('expert', 'hidden')
Inputs may be any that keep to these rules, and one draw needn't show every extreme that they name: `expert_ids`: each row names 8 different experts; in each aligned block of 64 rows no expert is named by more than 16 rows.
All inputs are finite; a program needn't handle non-finite values.
Results may differ from a plain program's by a relative error of at most 0.0057.
Values may be sent and summed in bfloat16 or wider, within the bound.
No kernel may reach another device: no remote copies, remote signals or barrier semaphores. Data moves between devices by JAX's collectives and lax.ppermute only.
A program may use at most 64 MiB of HBM per device.

v0:
```python
import jax
import jax.numpy as jnp
from jax import lax
from jax.sharding import PartitionSpec as P


def on_device(tokens, expert_ids, gate_weights, gate_proj, up_proj, down_proj):
    local_count = gate_proj.shape[0]
    experts_all = local_count * lax.axis_size("expert")
    tok_rows = tokens.shape[0]
    top_count = expert_ids.shape[1]
    capacity = 2 * tok_rows * top_count // experts_all
    flat_ids = expert_ids.reshape(-1)
    onehot = (flat_ids[:, None] == jnp.arange(experts_all, dtype=jnp.int32)[None, :]).astype(
        jnp.int32
    )
    slot_index = jnp.sum((jnp.cumsum(onehot, axis=0) - onehot) * onehot, axis=1)
    position = flat_ids * capacity + slot_index
    token_of = jnp.arange(tok_rows * top_count, dtype=jnp.int32) // top_count
    full_rows = lax.all_gather(tokens, "hidden", axis=1, tiled=True)
    packed = jnp.zeros((experts_all * capacity, full_rows.shape[1]), full_rows.dtype)
    packed = packed.at[position].set(full_rows[token_of])
    arrived = lax.all_to_all(
        packed.reshape(experts_all, capacity, full_rows.shape[1]),
        "expert",
        split_axis=0,
        concat_axis=1,
        tiled=True,
    )
    gate_sum = jnp.einsum("lrd,lfd->lfr", arrived, gate_proj, preferred_element_type=jnp.float32)
    up_sum = jnp.einsum("lrd,lfd->lfr", arrived, up_proj, preferred_element_type=jnp.float32)
    activation = (jax.nn.silu(gate_sum) * up_sum).astype(jnp.bfloat16)
    expert_out = jnp.einsum(
        "lfr,lfd->lrd",
        lax.all_gather(activation, "hidden", axis=1, tiled=True),
        down_proj,
        preferred_element_type=jnp.float32,
    ).astype(jnp.bfloat16)
    returned = lax.all_to_all(expert_out, "expert", split_axis=1, concat_axis=0, tiled=True)
    gathered = returned.reshape(experts_all * capacity, returned.shape[2])[position]
    gathered = gathered.reshape(tok_rows, top_count, returned.shape[2]).astype(jnp.float32)
    mixed = jnp.sum(gathered * gate_weights[:, :, None], axis=1)
    return mixed.astype(jnp.bfloat16)


def solution(mesh):
    in_specs = (
        P("expert", "hidden"),
        P("expert", None),
        P("expert", None),
        P("expert", "hidden", None),
        P("expert", "hidden", None),
        P("expert", None, "hidden"),
    )
    out_specs = P("expert", "hidden")
    return jax.shard_map(
        on_device, mesh=mesh, in_specs=in_specs, out_specs=out_specs, check_vma=False
    )
```

profile of v0, /device:TPU:1, one launch (start us, length us, event | category | flops | bytes accessed | tf_op | source)
XLA Modules:
  0.0 375.7 jit_solution(17025929349063810798)
XLA Ops:
  6.5 0.0 copy-start
  6.5 0.0 all-gather.3.cloned.1.call-start
  6.5 0.9 copy.20
  7.4 0.1 eq.29
  7.5 0.1 eq.25
  7.6 0.7 broadcast_multiply_fusion
  8.3 1.2 reduce-window.6
  9.5 0.2 slice_reduce_fusion
  9.8 0.1 copy.19
  9.9 0.1 mul.38
  10.0 27.1 %all_gather.6 = bf16[64,4096]{1,0:T(8,128)(2,1)S(1)} all-gather(bf16[64,512]{1,0:T(8,128)(2,1)} %param.6), channel_id=1, replica_groups=mesh['expert'=64,'hidden'=8] {'hidden'}, dimensions={1}, use_global_device_ids=true | all-gather | bytes 589824 | tf_op jit(solution)/shard_map/all_gather | solution.py:20
  37.1 0.1 fusion.29
  37.3 4.4 %gather_fusion = bf16[512,4096]{1,0:T(8,128)(2,1)} fusion(bf16[64,4096]{1,0:T(8,128)(2,1)S(1)} %all_gather.6, s32[1024]{0:T(1024)S(1)} %pad_clamp_fusion.1), kind=kCustom, calls=%fused_computation | custom fusion | bytes 8390656 | tf_op jit(solution)/shard_map/gather | solution.py:22
  41.6 12.4 %scatter_custom_fusion = bf16[1024,4096]{1,0:T(8,128)(2,1)} fusion(s32[512]{0:T(512)S(1)} %bitcast.75, bf16[512,4096]{1,0:T(8,128)(2,1)} %gather_fusion, bf16[]{:T(256)} %constant.26.clone.1), kind=kCustom, calls=%fused_computation.3 | custom fusion | bytes 8389120 | tf_op jit(solution)/shard_map/scatter | solution.py:22
  54.1 0.0 copy-start.2
  54.1 201.0 %all_to_all.8 = bf16[64,16,4096]{2,1,0:T(8,128)(2,1)S(1)} all-to-all(bf16[64,16,4096]{2,1,0:T(8,128)(2,1)} %bitcast.68), channel_id=1, replica_groups=mesh['expert'=64,'hidden'=8] {'expert'}, dimensions={0} | all-to-all | bytes 16777216 | tf_op jit(solution)/shard_map/all_to_all | solution.py:23
  255.0 0.0 copy-done.2
  255.0 0.0 copy-start.3
  255.0 2.9 fusion.14
  258.0 0.0 copy-done.3
  258.0 3.7 fusion.23
  261.7 0.0 all-gather.3.cloned.1.call-update
  261.7 43.4 %all-gather.3.cloned.1.call-done = bf16[1536,1024]{1,0:T(8,128)(2,1)} async-done(((bf16[192,1024]{1,0:T(8,128)(2,1)}), bf16[1536,1024]{1,0:T(8,128)(2,1)}) %all-gather.3.cloned.1.call-update) | async-done | bytes 3145744 | tf_op jit(solution)/shard_map/all_gather | solution.py:35
  305.1 0.0 copy-done
  305.1 3.7 fusion.11
  308.8 3.0 copy.31
  311.8 0.0 copy-start.1
  311.8 0.5 broadcast.125
  312.3 8.3 %reduce.2 = bf16[1024,512]{1,0:T(8,128)(2,1)S(1)} reduce(bf16[1024,1,512]{2,1,0:T(2,128)(2,1)} %bitcast.73, bf16[]{:T(256)} %broadcast.125), dimensions={1}, to_apply=%bitcast.67.reduce_sub_computation | reduce | bytes 2097154
  320.6 1.6 reshape.173
  322.2 10.3 %all-to-all-start.1 = ((bf16[64,2,4096]{2,1,0:T(2,128)(2,1)}), bf16[64,2,4096]{2,1,0:T(2,128)(2,1)S(1)}, u32[]{:S(2)}, u32[]{:S(2)}) async-start(bf16[64,2,4096]{2,1,0:T(2,128)(2,1)} %reshape.173), calls=%async_computation.1 | async-start | bytes 2097152 | tf_op jit(solution)/shard_map/all_to_all | solution.py:39
  332.5 0.0 copy-done.1
  332.5 0.1 copy.24
  332.6 27.9 %all-to-all-done.1 = bf16[64,2,4096]{2,1,0:T(2,128)(2,1)S(1)} async-done(((bf16[64,2,4096]{2,1,0:T(2,128)(2,1)}), bf16[64,2,4096]{2,1,0:T(2,128)(2,1)S(1)}, u32[]{:S(2)}, u32[]{:S(2)}) %all-to-all-start.1) | async-done | bytes 1048608 | tf_op jit(solution)/shard_map/all_to_all | solution.py:39
  360.5 3.5 reshape.174
  364.0 1.9 copy.30
  365.9 2.0 gather_fusion.1
  367.8 1.0 fusion.26
  (7 shorter events, 0.1 us)
Async XLA Ops:
  6.5 298.6 %copy-start = (bf16[1,1536,512]{2,1,0:T(8,128)(2,1)S(1)}, bf16[1,1536,512]{2,1,0:T(8,128)(2,1)}, u32[]{:S(2)}) copy-start(bf16[1,1536,512]{2,1,0:T(8,128)(2,1)} %param.11) | copy-start | bytes 4718596
  6.5 298.6 %all-gather.3.cloned.1.call-start = ((), (), s32[]{:S(2)}) async-start(), calls=%async_computation.2 | async-start | bytes 3538944 | tf_op jit(solution)/shard_map/all_gather | solution.py:35
  54.1 201.0 %copy-start.2 = (bf16[1,192,4096]{2,1,0:T(8,128)(2,1)S(1)}, bf16[1,192,4096]{2,1,0:T(8,128)(2,1)}, u32[]{:S(2)}) copy-start(bf16[1,192,4096]{2,1,0:T(8,128)(2,1)} %param.9) | copy-start | bytes 4718596
  255.0 2.9 copy-start.3
  311.8 20.7 %copy-start.1 = (f32[64,8]{0,1:T(8,128)S(1)}, f32[64,8]{0,1:T(8,128)}, u32[]{:S(2)}) copy-start(f32[64,8]{0,1:T(8,128)} %param.8) | copy-start | bytes 6148
  322.2 38.3 %all-to-all-start.1 = ((bf16[64,2,4096]{2,1,0:T(2,128)(2,1)}), bf16[64,2,4096]{2,1,0:T(2,128)(2,1)S(1)}, u32[]{:S(2)}, u32[]{:S(2)}) async-start(bf16[64,2,4096]{2,1,0:T(2,128)(2,1)} %reshape.173), calls=%async_computation.1 | async-start | bytes 2097152 | tf_op jit(solution)/shard_map/all_to_all | solution.py:39
Sparse Core Ops, SparseCore 0:
  261.8 43.2 all-gather.2
where the time goes:
time: 376 us
  blocking collectives  228 us (61%)
  waiting for transfers between devices  71.3 us (19%)
  local copies, waits for them, and re-layouts  30.8 us (8%)
  between operations  13.5 us (4%)
  other arithmetic  11.3 us (3%)
  starting transfers between devices  10.4 us (3%)
  matrix products  10.3 us (3%)
    all_to_all x1, blocking collectives, on_device(): lax.all_to_all(packed.reshape(experts_all, capacity, full_rows.shape[1]),...  201 us
    all_gather x1, waiting for transfers between devices, on_device(): lax.all_gather(activation, 'hidden', axis=1, tiled=True)  43.4 us
    all_to_all x1, waiting for transfers between devices, on_device(): lax.all_to_all(expert_out, 'expert', split_axis=1, concat_axis=0, tiled=T...  27.9 us
    all_gather x1, blocking collectives, on_device(): full_rows = lax.all_gather(tokens, 'hidden', axis=1, tiled=True)  27.1 us
    scatter x1, local copies, waits for them, and re-layouts, on_device(): packed = packed.at[position].set(full_rows[token_of])  12.4 us
    all_to_all x1, starting transfers between devices, on_device(): lax.all_to_all(expert_out, 'expert', split_axis=1, concat_axis=0, tiled=T...  10.3 us
    unnamed x14, local copies, waits for them, and re-layouts  8.43 us
    unnamed x1, other arithmetic  8.25 us
  transfers between devices with their start and end apart: 2, of which 2 were waited for; matrix products, arithmetic and copies ran while one was open for 0% of the time, Pallas kernels for 0%

commit v1 on v0

--- a/solution.py
+++ b/solution.py
@@ -30,11 +30,28 @@
     gate_sum = jnp.einsum("lrd,lfd->lfr", arrived, gate_proj, preferred_element_type=jnp.float32)
     up_sum = jnp.einsum("lrd,lfd->lfr", arrived, up_proj, preferred_element_type=jnp.float32)
     activation = (jax.nn.silu(gate_sum) * up_sum).astype(jnp.bfloat16)
-    expert_out = jnp.einsum(
-        "lfr,lfd->lrd",
-        lax.all_gather(activation, "hidden", axis=1, tiled=True),
-        down_proj,
-        preferred_element_type=jnp.float32,
+
+    def create_shapes_all(buf, mesh_name, dim_k, here_x):
+        front, response = (lax.psum(1, axis_name=mesh_name), lax.axis_index(mesh_name))
+        inbox = [(src_i, (src_i - 1) % front) for src_i in range(front)]
+        k_now = buf.shape[dim_k]
+        outer = buf
+        e_now = here_x(outer, response * k_now)
+        for j in range(1, front):
+            outer = lax.ppermute(outer, perm=inbox, axis_name=mesh_name)
+            e_now = e_now + here_x(outer, (response + j) % front * k_now)
+        return e_now
+
+    expert_out = create_shapes_all(
+        activation,
+        "hidden",
+        1,
+        here_x=lambda part, at: jnp.einsum(
+            "lfr,lfd->lrd",
+            part,
+            lax.dynamic_slice_in_dim(down_proj, at, part.shape[1], axis=1),
+            preferred_element_type=jnp.float32,
+        ),
     ).astype(jnp.bfloat16)
     returned = lax.all_to_all(expert_out, "expert", split_axis=1, concat_axis=0, tiled=True)
     gathered = returned.reshape(experts_all * capacity, returned.shape[2])[position]

time: 376 us -> 398 us (1.059)
  starting transfers between devices: 10.4 us -> 53.8 us
  between operations: 13.5 us -> 0.29 us
  waiting for transfers between devices: 71.3 us -> 62.8 us
    all_gather x1 -> x0, waiting for transfers between devices: 43.4 us -> none  [on_device(): lax.all_gather(activation, 'hidden', axis=1, tiled=True)]
    ppermute x0 -> x7, starting transfers between devices: none -> 35.5 us  [create_shapes_all(): outer = lax.ppermute(outer, perm=inbox, axis_name=mesh_name)]
    ppermute x0 -> x7, waiting for transfers between devices: none -> 34.9 us  [create_shapes_all(): outer = lax.ppermute(outer, perm=inbox, axis_name=mesh_name)]
    all_to_all x1, starting transfers between devices: 10.3 us -> 18.3 us  [on_device(): lax.all_to_all(expert_out, 'expert', split_axis=1, concat_axis=0, tiled=T...]
  transfers between devices with their start and end apart: 2 -> 8, of which waited for: 2 -> 8; matrix products, arithmetic and copies ran while one was open for 0% -> 1% of each run, Pallas kernels for 0% -> 0%
where the time goes in v1:
time: 398 us; the launch traced here: 397 us
  blocking collectives  228 us (57%)
  waiting for transfers between devices  62.8 us (16%)
  starting transfers between devices  53.8 us (14%)
  local copies, waits for them, and re-layouts  30.6 us (8%)
  other arithmetic  11.2 us (3%)
  matrix products  10 us (3%)
    all_to_all x1, blocking collectives, on_device(): lax.all_to_all(packed.reshape(experts_all, capacity, full_rows.shape[1]),...  201 us
    ppermute x7, starting transfers between devices, create_shapes_all(): outer = lax.ppermute(outer, perm=inbox, axis_name=mesh_name)  35.5 us
    ppermute x7, waiting for transfers between devices, create_shapes_all(): outer = lax.ppermute(outer, perm=inbox, axis_name=mesh_name)  34.9 us
    all_to_all x1, waiting for transfers between devices, on_device(): lax.all_to_all(expert_out, 'expert', split_axis=1, concat_axis=0, tiled=T...  27.9 us
    all_gather x1, blocking collectives, on_device(): full_rows = lax.all_gather(tokens, 'hidden', axis=1, tiled=True)  27.1 us
    all_to_all x1, starting transfers between devices, on_device(): lax.all_to_all(expert_out, 'expert', split_axis=1, concat_axis=0, tiled=T...  18.3 us
    scatter x1, local copies, waits for them, and re-layouts, on_device(): packed = packed.at[position].set(full_rows[token_of])  12.4 us
    unnamed x14, local copies, waits for them, and re-layouts  8.31 us
  transfers between devices with their start and end apart: 8, of which 8 were waited for; matrix products, arithmetic and copies ran while one was open for 1% of the time, Pallas kernels for 0%

profile of v1, /device:TPU:1, one launch (start us, length us, event | category | flops | bytes accessed | tf_op | source)
XLA Modules:
  0.0 397.1 jit_solution(5548831401026045196)
XLA Ops:
  0.0 0.0 copy-start
  0.0 0.8 broadcast_multiply_fusion
  0.8 0.8 copy.20
  1.6 0.1 eq.33
  1.7 0.1 eq.37
  1.8 0.1 copy.19
  1.9 0.1 mul.62
  2.0 1.2 reduce-window.6
  3.2 0.2 slice_reduce_fusion
  3.5 27.1 %all_gather.3 = bf16[64,4096]{1,0:T(8,128)(2,1)S(1)} all-gather(bf16[64,512]{1,0:T(8,128)(2,1)} %param.6), channel_id=1, replica_groups=mesh['expert'=64,'hidden'=8] {'hidden'}, dimensions={1}, use_global_device_ids=true | all-gather | bytes 589824 | tf_op jit(solution)/shard_map/all_gather | solution.py:20
  30.6 0.1 fusion.52
  30.7 4.4 %gather_fusion = bf16[512,4096]{1,0:T(8,128)(2,1)} fusion(bf16[64,4096]{1,0:T(8,128)(2,1)S(1)} %all_gather.3, s32[1024]{0:T(1024)S(1)} %pad_clamp_fusion.1), kind=kCustom, calls=%fused_computation | custom fusion | bytes 8390656 | tf_op jit(solution)/shard_map/gather | solution.py:22
  35.1 12.4 %scatter_custom_fusion = bf16[1024,4096]{1,0:T(8,128)(2,1)} fusion(s32[512]{0:T(512)S(1)} %bitcast.115, bf16[512,4096]{1,0:T(8,128)(2,1)} %gather_fusion, bf16[]{:T(256)} %constant.71.clone.1), kind=kCustom, calls=%fused_computation.3 | custom fusion | bytes 8389120 | tf_op jit(solution)/shard_map/scatter | solution.py:22
  47.5 0.0 copy-start.2
  47.5 201.1 %all_to_all.8 = bf16[64,16,4096]{2,1,0:T(8,128)(2,1)S(1)} all-to-all(bf16[64,16,4096]{2,1,0:T(8,128)(2,1)} %bitcast.107), channel_id=1, replica_groups=mesh['expert'=64,'hidden'=8] {'expert'}, dimensions={0} | all-to-all | bytes 16777216 | tf_op jit(solution)/shard_map/all_to_all | solution.py:23
  248.7 0.0 copy-done.2
  248.7 0.0 copy-start.3
  248.7 2.9 fusion.7
  251.6 0.0 copy-done.3
  251.6 2.9 fusion.16
  254.5 4.6 %collective-permute-start = (bf16[1,192,1024]{2,1,0:T(8,128)(2,1)S(1)}, bf16[1,192,1024]{2,1,0:T(8,128)(2,1)S(1)}, u32[]{:S(2)}, u32[]{:S(2)}) collective-permute-start(bf16[1,192,1024]{2,1,0:T(8,128)(2,1)S(1)} %bitcast.113), channel_id=1, source_target_pairs={{0,7},{1,0},{2,1},{3,2},{4,3},{5,4},{6,5},{7,6},{8,15},{9,8},{10,9... | collective-permute-start | bytes 1179656 | tf_op jit(solution)/shard_map/ppermute | solution.py:41
  259.2 6.2 %collective-permute-done = bf16[1,192,1024]{2,1,0:T(8,128)(2,1)S(1)} collective-permute-done((bf16[1,192,1024]{2,1,0:T(8,128)(2,1)S(1)}, bf16[1,192,1024]{2,1,0:T(8,128)(2,1)S(1)}, u32[]{:S(2)}, u32[]{:S(2)}) %collective-permute-start) | collective-permute-done | bytes 393248 | tf_op jit(solution)/shard_map/ppermute | solution.py:41
  265.4 5.3 %collective-permute-start.1 = (bf16[1,192,1024]{2,1,0:T(8,128)(2,1)S(1)}, bf16[1,192,1024]{2,1,0:T(8,128)(2,1)S(1)}, u32[]{:S(2)}, u32[]{:S(2)}) collective-permute-start(bf16[1,192,1024]{2,1,0:T(8,128)(2,1)S(1)} %collective-permute-done), channel_id=1, source_target_pairs={{0,7},{1,0},{2,1},{3,2},{4,3},{5,4},{6,5},{7,6},{8,15},{9,8},{10,9... | collective-permute-start | bytes 1179656 | tf_op jit(solution)/shard_map/ppermute | solution.py:41
  270.7 5.3 %collective-permute-done.1 = bf16[1,192,1024]{2,1,0:T(8,128)(2,1)S(1)} collective-permute-done((bf16[1,192,1024]{2,1,0:T(8,128)(2,1)S(1)}, bf16[1,192,1024]{2,1,0:T(8,128)(2,1)S(1)}, u32[]{:S(2)}, u32[]{:S(2)}) %collective-permute-start.1) | collective-permute-done | bytes 393248 | tf_op jit(solution)/shard_map/ppermute | solution.py:41
  276.1 5.3 %collective-permute-start.2 = (bf16[1,192,1024]{2,1,0:T(8,128)(2,1)S(1)}, bf16[1,192,1024]{2,1,0:T(8,128)(2,1)S(1)}, u32[]{:S(2)}, u32[]{:S(2)}) collective-permute-start(bf16[1,192,1024]{2,1,0:T(8,128)(2,1)S(1)} %collective-permute-done.1), channel_id=1, source_target_pairs={{0,7},{1,0},{2,1},{3,2},{4,3},{5,4},{6,5},{7,6},{8,15},{9,8},{10,9... | collective-permute-start | bytes 1179656 | tf_op jit(solution)/shard_map/ppermute | solution.py:41
  281.4 4.7 %collective-permute-done.2 = bf16[1,192,1024]{2,1,0:T(8,128)(2,1)S(1)} collective-permute-done((bf16[1,192,1024]{2,1,0:T(8,128)(2,1)S(1)}, bf16[1,192,1024]{2,1,0:T(8,128)(2,1)S(1)}, u32[]{:S(2)}, u32[]{:S(2)}) %collective-permute-start.2) | collective-permute-done | bytes 393248 | tf_op jit(solution)/shard_map/ppermute | solution.py:41
  286.1 5.0 %collective-permute-start.3 = (bf16[1,192,1024]{2,1,0:T(8,128)(2,1)S(1)}, bf16[1,192,1024]{2,1,0:T(8,128)(2,1)S(1)}, u32[]{:S(2)}, u32[]{:S(2)}) collective-permute-start(bf16[1,192,1024]{2,1,0:T(8,128)(2,1)S(1)} %collective-permute-done.2), channel_id=1, source_target_pairs={{0,7},{1,0},{2,1},{3,2},{4,3},{5,4},{6,5},{7,6},{8,15},{9,8},{10,9... | collective-permute-start | bytes 1179656 | tf_op jit(solution)/shard_map/ppermute | solution.py:41
  291.2 0.0 copy-done
  291.2 0.5 fusion.40
  291.7 4.1 %collective-permute-done.3 = bf16[1,192,1024]{2,1,0:T(8,128)(2,1)S(1)} collective-permute-done((bf16[1,192,1024]{2,1,0:T(8,128)(2,1)S(1)}, bf16[1,192,1024]{2,1,0:T(8,128)(2,1)S(1)}, u32[]{:S(2)}, u32[]{:S(2)}) %collective-permute-start.3) | collective-permute-done | bytes 393248 | tf_op jit(solution)/shard_map/ppermute | solution.py:41
  295.8 5.0 %collective-permute-start.4 = (bf16[1,192,1024]{2,1,0:T(8,128)(2,1)S(1)}, bf16[1,192,1024]{2,1,0:T(8,128)(2,1)S(1)}, u32[]{:S(2)}, u32[]{:S(2)}) collective-permute-start(bf16[1,192,1024]{2,1,0:T(8,128)(2,1)S(1)} %collective-permute-done.3), channel_id=1, source_target_pairs={{0,7},{1,0},{2,1},{3,2},{4,3},{5,4},{6,5},{7,6},{8,15},{9,8},{10,9... | collective-permute-start | bytes 1179656 | tf_op jit(solution)/shard_map/ppermute | solution.py:41
  300.8 0.5 fusion.31
  301.3 0.5 fusion.29
  301.8 3.8 collective-permute-done.4
  305.6 5.0 %collective-permute-start.5 = (bf16[1,192,1024]{2,1,0:T(8,128)(2,1)S(1)}, bf16[1,192,1024]{2,1,0:T(8,128)(2,1)S(1)}, u32[]{:S(2)}, u32[]{:S(2)}) collective-permute-start(bf16[1,192,1024]{2,1,0:T(8,128)(2,1)S(1)} %collective-permute-done.4), channel_id=1, source_target_pairs={{0,7},{1,0},{2,1},{3,2},{4,3},{5,4},{6,5},{7,6},{8,15},{9,8},{10,9... | collective-permute-start | bytes 1179656 | tf_op jit(solution)/shard_map/ppermute | solution.py:41
  310.6 0.5 fusion.27
  311.1 0.5 fusion.25
  311.6 4.9 %collective-permute-done.5 = bf16[1,192,1024]{2,1,0:T(8,128)(2,1)S(1)} collective-permute-done((bf16[1,192,1024]{2,1,0:T(8,128)(2,1)S(1)}, bf16[1,192,1024]{2,1,0:T(8,128)(2,1)S(1)}, u32[]{:S(2)}, u32[]{:S(2)}) %collective-permute-start.5) | collective-permute-done | bytes 393248 | tf_op jit(solution)/shard_map/ppermute | solution.py:41
  316.5 5.2 %collective-permute-start.6 = (bf16[1,192,1024]{2,1,0:T(8,128)(2,1)S(1)}, bf16[1,192,1024]{2,1,0:T(8,128)(2,1)S(1)}, u32[]{:S(2)}, u32[]{:S(2)}) collective-permute-start(bf16[1,192,1024]{2,1,0:T(8,128)(2,1)S(1)} %collective-permute-done.5), channel_id=1, source_target_pairs={{0,7},{1,0},{2,1},{3,2},{4,3},{5,4},{6,5},{7,6},{8,15},{9,8},{10,9... | collective-permute-start | bytes 1179656 | tf_op jit(solution)/shard_map/ppermute | solution.py:41
  321.7 0.5 fusion.23
  322.2 0.5 fusion.21
  322.7 5.8 %collective-permute-done.6 = bf16[1,192,1024]{2,1,0:T(8,128)(2,1)S(1)} collective-permute-done((bf16[1,192,1024]{2,1,0:T(8,128)(2,1)S(1)}, bf16[1,192,1024]{2,1,0:T(8,128)(2,1)S(1)}, u32[]{:S(2)}, u32[]{:S(2)}) %collective-permute-start.6) | collective-permute-done | bytes 393248 | tf_op jit(solution)/shard_map/ppermute | solution.py:41
  328.4 0.8 fusion.6
  329.3 3.0 copy.31
  332.3 0.5 broadcast.136
  332.8 8.0 %reduce.2 = bf16[1024,512]{1,0:T(8,128)(2,1)S(1)} reduce(bf16[1024,1,512]{2,1,0:T(2,128)(2,1)} %bitcast.112, bf16[]{:T(256)} %broadcast.136), dimensions={1}, to_apply=%bitcast.106.reduce_sub_computation | reduce | bytes 2097154
  340.8 0.0 copy-start.1
  340.8 1.6 reshape.239
  342.4 18.3 %all-to-all-start.1 = ((bf16[64,2,4096]{2,1,0:T(2,128)(2,1)}), bf16[64,2,4096]{2,1,0:T(2,128)(2,1)S(1)}, u32[]{:S(2)}, u32[]{:S(2)}) async-start(bf16[64,2,4096]{2,1,0:T(2,128)(2,1)} %reshape.239), calls=%async_computation.1 | async-start | bytes 2097152 | tf_op jit(solution)/shard_map/all_to_all | solution.py:56
  360.8 0.0 copy-done.1
  360.8 0.1 copy.24
  360.9 27.9 %all-to-all-done.1 = bf16[64,2,4096]{2,1,0:T(2,128)(2,1)S(1)} async-done(((bf16[64,2,4096]{2,1,0:T(2,128)(2,1)}), bf16[64,2,4096]{2,1,0:T(2,128)(2,1)S(1)}, u32[]{:S(2)}, u32[]{:S(2)}) %all-to-all-start.1) | async-done | bytes 1048608 | tf_op jit(solution)/shard_map/all_to_all | solution.py:56
  388.8 3.5 reshape.240
  392.2 1.9 copy.30
  394.1 2.0 gather_fusion.1
  396.1 1.0 fusion.19
  (7 shorter events, 0.1 us)
Async XLA Ops:
  0.0 291.2 %copy-start = (bf16[1,1536,512]{2,1,0:T(8,128)(2,1)S(1)}, bf16[1,1536,512]{2,1,0:T(8,128)(2,1)}, u32[]{:S(2)}) copy-start(bf16[1,1536,512]{2,1,0:T(8,128)(2,1)} %param.11) | copy-start | bytes 4718596
  47.5 201.1 %copy-start.2 = (bf16[1,192,4096]{2,1,0:T(8,128)(2,1)S(1)}, bf16[1,192,4096]{2,1,0:T(8,128)(2,1)}, u32[]{:S(2)}) copy-start(bf16[1,192,4096]{2,1,0:T(8,128)(2,1)} %param.9) | copy-start | bytes 4718596
  248.7 2.9 copy-start.3
  254.5 10.9 %collective-permute-start = (bf16[1,192,1024]{2,1,0:T(8,128)(2,1)S(1)}, bf16[1,192,1024]{2,1,0:T(8,128)(2,1)S(1)}, u32[]{:S(2)}, u32[]{:S(2)}) collective-permute-start(bf16[1,192,1024]{2,1,0:T(8,128)(2,1)S(1)} %bitcast.113), channel_id=1, source_target_pairs={{0,7},{1,0},{2,1},{3,2},{4,3},{5,4},{6,5},{7,6},{8,15},{9,8},{10,9... | collective-permute-start | bytes 1179656 | tf_op jit(solution)/shard_map/ppermute | solution.py:41
  265.4 10.6 %collective-permute-start.1 = (bf16[1,192,1024]{2,1,0:T(8,128)(2,1)S(1)}, bf16[1,192,1024]{2,1,0:T(8,128)(2,1)S(1)}, u32[]{:S(2)}, u32[]{:S(2)}) collective-permute-start(bf16[1,192,1024]{2,1,0:T(8,128)(2,1)S(1)} %collective-permute-done), channel_id=1, source_target_pairs={{0,7},{1,0},{2,1},{3,2},{4,3},{5,4},{6,5},{7,6},{8,15},{9,8},{10,9... | collective-permute-start | bytes 1179656 | tf_op jit(solution)/shard_map/ppermute | solution.py:41
  276.1 10.0 %collective-permute-start.2 = (bf16[1,192,1024]{2,1,0:T(8,128)(2,1)S(1)}, bf16[1,192,1024]{2,1,0:T(8,128)(2,1)S(1)}, u32[]{:S(2)}, u32[]{:S(2)}) collective-permute-start(bf16[1,192,1024]{2,1,0:T(8,128)(2,1)S(1)} %collective-permute-done.1), channel_id=1, source_target_pairs={{0,7},{1,0},{2,1},{3,2},{4,3},{5,4},{6,5},{7,6},{8,15},{9,8},{10,9... | collective-permute-start | bytes 1179656 | tf_op jit(solution)/shard_map/ppermute | solution.py:41
  286.1 9.7 %collective-permute-start.3 = (bf16[1,192,1024]{2,1,0:T(8,128)(2,1)S(1)}, bf16[1,192,1024]{2,1,0:T(8,128)(2,1)S(1)}, u32[]{:S(2)}, u32[]{:S(2)}) collective-permute-start(bf16[1,192,1024]{2,1,0:T(8,128)(2,1)S(1)} %collective-permute-done.2), channel_id=1, source_target_pairs={{0,7},{1,0},{2,1},{3,2},{4,3},{5,4},{6,5},{7,6},{8,15},{9,8},{10,9... | collective-permute-start | bytes 1179656 | tf_op jit(solution)/shard_map/ppermute | solution.py:41
  295.8 9.8 %collective-permute-start.4 = (bf16[1,192,1024]{2,1,0:T(8,128)(2,1)S(1)}, bf16[1,192,1024]{2,1,0:T(8,128)(2,1)S(1)}, u32[]{:S(2)}, u32[]{:S(2)}) collective-permute-start(bf16[1,192,1024]{2,1,0:T(8,128)(2,1)S(1)} %collective-permute-done.3), channel_id=1, source_target_pairs={{0,7},{1,0},{2,1},{3,2},{4,3},{5,4},{6,5},{7,6},{8,15},{9,8},{10,9... | collective-permute-start | bytes 1179656 | tf_op jit(solution)/shard_map/ppermute | solution.py:41
  305.6 10.9 %collective-permute-start.5 = (bf16[1,192,1024]{2,1,0:T(8,128)(2,1)S(1)}, bf16[1,192,1024]{2,1,0:T(8,128)(2,1)S(1)}, u32[]{:S(2)}, u32[]{:S(2)}) collective-permute-start(bf16[1,192,1024]{2,1,0:T(8,128)(2,1)S(1)} %collective-permute-done.4), channel_id=1, source_target_pairs={{0,7},{1,0},{2,1},{3,2},{4,3},{5,4},{6,5},{7,6},{8,15},{9,8},{10,9... | collective-permute-start | bytes 1179656 | tf_op jit(solution)/shard_map/ppermute | solution.py:41
  316.5 12.0 %collective-permute-start.6 = (bf16[1,192,1024]{2,1,0:T(8,128)(2,1)S(1)}, bf16[1,192,1024]{2,1,0:T(8,128)(2,1)S(1)}, u32[]{:S(2)}, u32[]{:S(2)}) collective-permute-start(bf16[1,192,1024]{2,1,0:T(8,128)(2,1)S(1)} %collective-permute-done.5), channel_id=1, source_target_pairs={{0,7},{1,0},{2,1},{3,2},{4,3},{5,4},{6,5},{7,6},{8,15},{9,8},{10,9... | collective-permute-start | bytes 1179656 | tf_op jit(solution)/shard_map/ppermute | solution.py:41
  340.8 20.0 %copy-start.1 = (f32[64,8]{0,1:T(8,128)S(1)}, f32[64,8]{0,1:T(8,128)}, u32[]{:S(2)}) copy-start(f32[64,8]{0,1:T(8,128)} %param.8) | copy-start | bytes 6148
  342.4 46.3 %all-to-all-start.1 = ((bf16[64,2,4096]{2,1,0:T(2,128)(2,1)}), bf16[64,2,4096]{2,1,0:T(2,128)(2,1)S(1)}, u32[]{:S(2)}, u32[]{:S(2)}) async-start(bf16[64,2,4096]{2,1,0:T(2,128)(2,1)} %reshape.239), calls=%async_computation.1 | async-start | bytes 2097152 | tf_op jit(solution)/shard_map/all_to_all | solution.py:56
